TPU v7x, 512 devices: a whole 4x8x8 slice. The times are simulated.
512 devices in a mesh: node: 32 (over z_lo, x, core), group: 16 (over y, z_hi).
Axes of the slice: x: 4, y: 8, z: 8 (z_hi: 2, z_lo: 4; z = z_hi * 4 + z_lo), core: 2. Of those that a mesh axis runs over, the one named last changes fastest.
Arguments:
- tokens: bfloat16 [131072, 1024], P(('node', 'group')), may hold values from -6 to 6
- grad_out: bfloat16 [131072, 1024], P(('node', 'group')), may hold values from -1.5 to 1.5
- router_gate: float32 [131072, 4], P(('node', 'group')), may hold values from 0.1 to 1
- counts: int32 [512], P(('node', 'group')), may hold values from 1 to 2
- routes: int32 [512, 2, 4], P(('node', 'group')), may hold values from 0 to 15, as said below
- partner: int32 [32], replicated, may hold values from 0 to 31, as said below
- w_gate: bfloat16 [512, 1024, 256], P(('node', 'group')), may hold values from -0.1875 to 0.1875
- w_up: bfloat16 [512, 1024, 256], P(('node', 'group')), may hold values from -0.1875 to 0.1875
- w_down: bfloat16 [512, 256, 1024], P(('node', 'group')), may hold values from -0.375 to 0.375
Outputs:
- grad_tokens: bfloat16 [131072, 1024], P(('node', 'group'))
- grad_gate: bfloat16 [512, 1024, 256], P(('node', 'group'))
- grad_up: bfloat16 [512, 1024, 256], P(('node', 'group'))
- grad_down: bfloat16 [512, 256, 1024], P(('node', 'group'))
Inputs may be any that keep to these rules, and one draw needn't show every extreme that they name: `routes`: the 8 entries of one device name different devices of its group; every device of a group is named; in every node group one device is named by exactly 12 entries and none by more. partner pairs the nodes: partner[partner[n]] = n and partner[n] != n.
All inputs are finite; a program needn't handle non-finite values.
Results may differ from a plain program's by a relative error of at most 0.015.
Values may be sent and summed in bfloat16 or wider, within the bound.
A program may use at most 128 MiB of HBM per device.

v0:
```python
import math
import jax
import jax.numpy as jnp
from jax import lax
from jax.sharding import PartitionSpec as P


def side_by_side(arrays, axis, split_dim, concat_dim, along):
    widths = [math.prod(a.shape[along:]) for a in arrays]
    both = jnp.concatenate(
        [a.reshape(*a.shape[:along], w) for a, w in zip(arrays, widths)], axis=along
    )
    result = lax.all_to_all(both, axis, split_axis=split_dim, concat_axis=concat_dim, tiled=True)
    tiles = jnp.split(result, [sum(widths[:k]) for k in range(1, len(widths))], axis=along)
    return tuple(
        (b.reshape(*result.shape[:along], *a.shape[along:]) for a, b in zip(arrays, tiles))
    )


def sent_to_all(x, axis):
    copies = jnp.broadcast_to(x, (lax.axis_size(axis), *x.shape))
    return lax.all_to_all(copies, axis, split_axis=0, concat_axis=0, tiled=True)


def in_order(tiles, dim):
    tiles = jnp.moveaxis(tiles, 0, dim)
    dims = tiles.shape
    return tiles.reshape(*dims[:dim], dims[dim] * dims[dim + 1], *dims[dim + 2 :])


def gathered_copies(x, axis, dim):
    tiles = sent_to_all(x, axis)
    return in_order(tiles, dim)


def against(left, right):
    return lax.dot_general(
        left, right, (((1,), (1,)), ((), ())), preferred_element_type=jnp.float32
    )


def across(left, right):
    return lax.dot_general(
        left, right, (((0,), (0,)), ((), ())), preferred_element_type=jnp.float32
    )


def forward_pass(rows, w_gate, w_up):
    gate_pre = jnp.dot(rows, w_gate, preferred_element_type=jnp.float32)
    up_pre = jnp.dot(rows, w_up, preferred_element_type=jnp.float32)
    sigmoid = jax.nn.sigmoid(gate_pre)
    swish = gate_pre * sigmoid
    hidden = (swish * up_pre).astype(jnp.bfloat16)
    return (gate_pre, up_pre, sigmoid, swish, hidden)


def relocate(w_gate, w_up, w_down, partner):
    nodes = lax.axis_size("node")
    depth, width = (w_gate.shape[1], w_gate.shape[2])
    gate_parts = w_gate.reshape(nodes, depth // nodes, width)
    up_parts = w_up.reshape(nodes, depth // nodes, width)
    down_parts = w_down.reshape(nodes, width // nodes, depth)
    mixed = (
        lax.all_to_all(gate_parts, "node", split_axis=0, concat_axis=0, tiled=True),
        lax.all_to_all(up_parts, "node", split_axis=0, concat_axis=0, tiled=True),
        lax.all_to_all(down_parts, "node", split_axis=0, concat_axis=0, tiled=True),
    )
    gate_pick = jnp.take(mixed[0], partner, axis=0)
    up_pick = jnp.take(mixed[1], partner, axis=0)
    down_pick = jnp.take(mixed[2], partner, axis=0)
    placed = side_by_side((gate_pick, up_pick, down_pick), "node", 0, 0, 1)
    return (
        placed[0].reshape(depth, width),
        placed[1].reshape(depth, width),
        placed[2].reshape(width, depth),
    )


def on_device(tokens, grad_out, router_gate, counts, routes, partner, w_gate, w_up, w_down):
    group = lax.axis_size("group")
    slots_dev, topk = (routes.shape[1], routes.shape[2])
    spread = slots_dev * topk
    capacity = spread + spread // 2
    block = tokens.shape[0] // slots_dev
    depth = tokens.shape[1]
    shard_rows = slots_dev * block
    placed_gate, placed_up, placed_down = relocate(w_gate, w_up, w_down, partner)
    live_rows = (jnp.arange(shard_rows, dtype=jnp.int32) // block < counts[0])[:, None]
    masked_tok = jnp.where(live_rows, tokens, jnp.zeros((), jnp.bfloat16))
    masked_out = jnp.where(live_rows, grad_out, jnp.zeros((), jnp.bfloat16))
    table = gathered_copies(routes, "group", 0)
    myself = lax.axis_index("group")
    flat = table.reshape(group * spread)
    chosen = flat == myself
    index = jnp.argsort(jnp.where(chosen, 0, 1).astype(jnp.int32), stable=True)[:capacity]
    valid = chosen[index]
    sources = index // spread
    own_block = index % spread // topk
    column = index % topk
    targets = jnp.arange(group, dtype=jnp.int32)
    onehot = (routes[0][None, :, :] == targets[:, None, None]).astype(jnp.bfloat16)
    pick = ((sources[:, None] == targets[None, :]) & valid[:, None]).astype(jnp.bfloat16)
    wanted = sources * shard_rows + own_block * block
    column_hot = (jnp.arange(topk, dtype=jnp.int32)[None, :] == column[:, None]).astype(jnp.float32)
    empty = jnp.zeros((capacity, block, depth), jnp.bfloat16)
    tok_piece = lax.all_gather(masked_tok, "group", axis=0, tiled=True)
    out_piece = lax.all_gather(masked_out, "group", axis=0, tiled=True)
    gate_piece = lax.all_gather(
        router_gate.astype(jnp.bfloat16), "group", axis=0, tiled=True
    ).astype(jnp.float32)
    length = tok_piece.shape[0]
    inside = valid & (wanted >= 0) & (wanted + block <= length)
    offset = jnp.clip(wanted, 0, length - block)

    def take_one(where_at):
        return (
            lax.dynamic_slice_in_dim(tok_piece, where_at, block, 0),
            lax.dynamic_slice_in_dim(out_piece, where_at, block, 0),
            lax.dynamic_slice_in_dim(gate_piece, where_at, block, 0),
        )

    tok_sel, out_sel, gate_sel = jax.vmap(take_one)(offset)
    weight = jnp.sum(gate_sel * column_hot[:, None, :], axis=2)
    scaled_sel = (weight[:, :, None] * out_sel.astype(jnp.float32)).astype(jnp.bfloat16)
    keep = inside[:, None, None]
    got_tok = jnp.where(keep, tok_sel, empty)
    got_grad = jnp.where(keep, scaled_sel, empty)
    rows = got_tok.reshape(capacity * block, depth)
    grads = got_grad.reshape(capacity * block, depth)
    gate_pre, up_pre, sigmoid, swish, hidden = forward_pass(rows, placed_gate, placed_up)
    grad_hidden = against(grads, placed_down)
    grad_upre = (grad_hidden * swish).astype(jnp.bfloat16)
    grad_gpre = (grad_hidden * up_pre * sigmoid * (1.0 + gate_pre * (1.0 - sigmoid))).astype(
        jnp.bfloat16
    )
    grad_wg = across(rows, grad_gpre).astype(jnp.bfloat16)
    grad_wu = across(rows, grad_upre).astype(jnp.bfloat16)
    grad_wd = across(hidden, grads).astype(jnp.bfloat16)
    inputs_grad = (against(grad_gpre, placed_gate) + against(grad_upre, placed_up)).astype(
        jnp.bfloat16
    )
    slots = jnp.einsum(
        "rg,rsd->gsd",
        pick,
        inputs_grad.reshape(capacity, block, depth),
        preferred_element_type=jnp.float32,
    ).astype(jnp.bfloat16)
    returned = lax.all_to_all(slots, "group", split_axis=0, concat_axis=0, tiled=True)
    mine = jnp.einsum("gbk,gsd->bsd", onehot, returned, preferred_element_type=jnp.float32)
    mine = mine.astype(jnp.bfloat16).reshape(shard_rows, depth)
    grad_tokens = jnp.where(live_rows, mine, jnp.zeros((), jnp.bfloat16))
    width = placed_gate.shape[1]
    return (
        grad_tokens,
        grad_wg.reshape(1, depth, width),
        grad_wu.reshape(1, depth, width),
        grad_wd.reshape(1, width, depth),
    )


def solution(mesh):
    return jax.shard_map(
        on_device,
        mesh=mesh,
        in_specs=(
            P(("node", "group"), None),
            P(("node", "group"), None),
            P(("node", "group"), None),
            P(("node", "group")),
            P(("node", "group"), None, None),
            P(),
            P(("node", "group"), None, None),
            P(("node", "group"), None, None),
            P(("node", "group"), None, None),
        ),
        out_specs=(
            P(("node", "group"), None),
            P(("node", "group"), None, None),
            P(("node", "group"), None, None),
            P(("node", "group"), None, None),
        ),
        check_vma=False,
    )
```

profile of v0, /device:TPU:36, one launch (start us, length us, event | category | flops | bytes accessed | tf_op | source)
XLA Modules:
  0.0 643.8 jit_solution(11685429359600773166)
XLA Ops:
  8.0 2.3 broadcast_select_fusion.5
  11.1 22.8 %all_to_all.37 = s32[16,1,2,4]{3,2,1,0:T(2,128)S(1)} all-to-all(s32[16,1,2,4]{3,2,1,0:T(2,128)S(1)} %broadcast_in_dim.93), channel_id=1, replica_groups=mesh['node'=32,'group'=16] {'group'}, dimensions={0} | all-to-all | bytes 1024 | tf_op jit(solution)/shard_map/all_to_all | solution.py:22
  33.9 25.4 %all_to_all.38 = bf16[32,32,256]{2,1,0:T(8,128)(2,1)S(1)} all-to-all(bf16[32,32,256]{2,1,0:T(8,128)(2,1)S(1)} %bitcast.94), channel_id=1, replica_groups=mesh['node'=32,'group'=16] {'node'}, dimensions={0} | all-to-all | bytes 1048576 | tf_op jit(solution)/shard_map/all_to_all | solution.py:64
  59.3 6.5 %all-to-all-start.2 = ((bf16[32,32,256]{2,1,0:T(8,128)(2,1)}), bf16[32,32,256]{2,1,0:T(8,128)(2,1)S(1)}, u32[]{:S(2)}, u32[]{:S(2)}) async-start(bf16[32,32,256]{2,1,0:T(8,128)(2,1)} %bitcast.7), calls=%async_computation.2 | async-start | bytes 1048576 | tf_op jit(solution)/shard_map/all_to_all | solution.py:65
  65.8 52.1 %all_gather.9 = bf16[4096,4]{0,1:T(4,128)(2,1)S(1)} all-gather(bf16[256,4]{0,1:T(4,128)(2,1)S(1)} %convert_element_type.78), channel_id=1, replica_groups=mesh['node'=32,'group'=16] {'group'}, dimensions={0}, use_global_device_ids=true | all-gather | bytes 34816 | tf_op jit(solution)/shard_map/all_gather | solution.py:108
  118.2 11.6 %all-to-all-start.3 = ((bf16[32,8,1024]{2,1,0:T(8,128)(2,1)}), bf16[32,8,1024]{2,1,0:T(8,128)(2,1)S(1)}, u32[]{:S(2)}, u32[]{:S(2)}) async-start(bf16[32,8,1024]{2,1,0:T(8,128)(2,1)} %bitcast.8), calls=%async_computation.3 | async-start | bytes 1048576 | tf_op jit(solution)/shard_map/all_to_all | solution.py:66
  129.8 2.5 sort.17
  135.0 56.3 %all-to-all-done.3 = bf16[32,8,1024]{2,1,0:T(8,128)(2,1)S(1)} async-done(((bf16[32,8,1024]{2,1,0:T(8,128)(2,1)}), bf16[32,8,1024]{2,1,0:T(8,128)(2,1)S(1)}, u32[]{:S(2)}, u32[]{:S(2)}) %all-to-all-start.3) | async-done | bytes 524320 | tf_op jit(solution)/shard_map/all_to_all | solution.py:66
  192.9 1.9 reduce
  194.8 2.1 reshape.318
  196.9 5.2 all-to-all-start.4
  202.2 15.8 %while.3 = (s32[]{:T(128)}, f32[4096,4]{0,1:T(4,128)S(1)}, s32[12,2]{0,1:T(2,128)S(1)}, f32[12,128,4]{1,2,0:T(4,128)S(1)}, s32[]{:T(128)}) while((s32[]{:T(128)}, f32[4096,4]{0,1:T(4,128)S(1)}, s32[12,2]{0,1:T(2,128)S(1)}, f32[12,128,4]{1,2,0:T(4,128)S(1)}, s32[]{:T(128)}) %tuple.54), condition=%wide.while_cond, body=%wide.while_body.sunk | while | flops 2 | bytes 4193 | solution.py:119
  218.0 21.4 %all-to-all-done.4 = bf16[32,2,12288]{2,1,0:T(2,128)(2,1)} async-done(((bf16[32,2,12288]{2,1,0:T(2,128)(2,1)}), bf16[32,2,12288]{2,1,0:T(2,128)(2,1)}, u32[]{:S(2)}, u32[]{:S(2)}) %all-to-all-start.4) | async-done | bytes 1572896 | tf_op jit(solution)/shard_map/all_to_all | solution.py:13
  239.4 8.2 %reshape.319 = bf16[32,1,24576]{2,1,0:T(2,128)(2,1)S(1)} reshape(bf16[32,2,12288]{2,1,0:T(2,128)(2,1)} %all-to-all-done.4) | data formatting | bytes 3145728
  247.6 1.7 copy.41
  253.0 27.4 %while.4 = (s32[]{:T(128)}, bf16[4096,1024]{1,0:T(8,128)(2,1)}, s32[12,2]{0,1:T(2,128)S(1)}, bf16[12,128,1024]{2,1,0:T(8,128)(2,1)S(1)}, s32[]{:T(128)}) while((s32[]{:T(128)}, bf16[4096,1024]{1,0:T(8,128)(2,1)}, s32[12,2]{0,1:T(2,128)S(1)}, bf16[12,128,1024]{2,1,0:T(8,128)(2,1)S(1)}, s32[]{:T(128)}) %tuple.67), condition=%wide.while_cond.1, body=%wide.while_body.1.sunk | while | flops 2 | bytes 524385 | solution.py:118
  253.6 1.7 bitcast_dynamic-update-slice_fusion.7
  255.9 1.7 bitcast_dynamic-update-slice_fusion.7
  258.2 1.7 bitcast_dynamic-update-slice_fusion.7
  260.5 1.7 bitcast_dynamic-update-slice_fusion.7
  262.7 1.7 bitcast_dynamic-update-slice_fusion.7
  265.0 1.7 bitcast_dynamic-update-slice_fusion.7
  267.3 1.7 bitcast_dynamic-update-slice_fusion.7
  269.6 1.7 bitcast_dynamic-update-slice_fusion.7
  271.9 1.7 bitcast_dynamic-update-slice_fusion.7
  274.2 1.7 bitcast_dynamic-update-slice_fusion.7
  276.4 1.7 bitcast_dynamic-update-slice_fusion.7
  278.7 1.7 bitcast_dynamic-update-slice_fusion.7
  280.4 1.7 copy-done
  282.1 134.0 %all-gather.5.cloned.1.call-done = bf16[4096,1024]{1,0:T(8,128)(2,1)} async-done(((bf16[256,1024]{1,0:T(8,128)(2,1)}), bf16[4096,1024]{1,0:T(8,128)(2,1)}) %all-gather.5.cloned.1.call-update) | async-done | bytes 8388624 | tf_op jit(solution)/shard_map/all_gather | solution.py:106
  416.5 27.4 %while.5 = (s32[]{:T(128)}, bf16[4096,1024]{1,0:T(8,128)(2,1)}, s32[12,2]{0,1:T(2,128)S(1)}, bf16[12,128,1024]{2,1,0:T(8,128)(2,1)S(1)}, s32[]{:T(128)}) while((s32[]{:T(128)}, bf16[4096,1024]{1,0:T(8,128)(2,1)}, s32[12,2]{0,1:T(2,128)S(1)}, bf16[12,128,1024]{2,1,0:T(8,128)(2,1)S(1)}, s32[]{:T(128)}) %tuple.68), condition=%wide.while_cond.2, body=%wide.while_body.2.sunk | while | flops 2 | bytes 524385 | solution.py:117
  417.1 1.7 bitcast_dynamic-update-slice_fusion.8
  419.4 1.7 bitcast_dynamic-update-slice_fusion.8
  421.7 1.7 bitcast_dynamic-update-slice_fusion.8
  424.0 1.7 bitcast_dynamic-update-slice_fusion.8
  426.3 1.7 bitcast_dynamic-update-slice_fusion.8
  428.5 1.7 bitcast_dynamic-update-slice_fusion.8
  430.8 1.7 bitcast_dynamic-update-slice_fusion.8
  443.9 3.4 fusion.5
  453.5 2.5 fusion.7
  456.1 4.3 copy.25
  460.4 7.2 %all-to-all-start.5 = ((bf16[16,128,1024]{2,1,0:T(8,128)(2,1)}), bf16[16,128,1024]{2,1,0:T(8,128)(2,1)}, u32[]{:S(2)}, u32[]{:S(2)}) async-start(bf16[16,128,1024]{2,1,0:T(8,128)(2,1)} %copy.25), calls=%async_computation.5 | async-start | bytes 8388608 | tf_op jit(solution)/shard_map/all_to_all | solution.py:148
  467.8 3.1 fusion.6
  470.9 1.8 fusion.14
  472.7 1.8 fusion.15
  474.6 1.9 fusion.16
  476.5 154.7 %all-to-all-done.5 = bf16[16,128,1024]{2,1,0:T(8,128)(2,1)} async-done(((bf16[16,128,1024]{2,1,0:T(8,128)(2,1)}), bf16[16,128,1024]{2,1,0:T(8,128)(2,1)}, u32[]{:S(2)}, u32[]{:S(2)}) %all-to-all-start.5) | async-done | bytes 4194336 | tf_op jit(solution)/shard_map/all_to_all | solution.py:148
  631.2 4.7 fusion.11
  (171 shorter events, 55.0 us)
Async XLA Ops:
  7.2 3.9 copy-start.10
  7.2 26.7 %copy-start.7 = (bf16[1,1024,256]{2,1,0:T(8,128)(2,1)S(1)}, bf16[1,1024,256]{2,1,0:T(8,128)(2,1)}, u32[]{:S(2)}) copy-start(bf16[1,1024,256]{2,1,0:T(8,128)(2,1)} %param.17) | copy-start | bytes 1572868
  7.2 58.6 %copy-start.9 = (f32[256,4]{0,1:T(4,128)S(1)}, f32[256,4]{0,1:T(4,128)}, u32[]{:S(2)}) copy-start(f32[256,4]{0,1:T(4,128)} %param.13) | copy-start | bytes 12292
  7.2 110.8 %copy-start.11 = (s32[32]{0:T(128)S(1)}, s32[32]{0:T(128)}, u32[]{:S(2)}) copy-start(s32[32]{0:T(128)} %param.16) | copy-start | bytes 388
  7.2 245.4 %all-gather.3.cloned.1.call-start = ((), (), s32[]{:S(2)}) async-start(), calls=%async_computation.6 | async-start | bytes 8912896 | tf_op jit(solution)/shard_map/all_gather | solution.py:107
  10.3 405.8 %all-gather.5.cloned.1.call-start = ((), (), s32[]{:S(2)}) async-start(), calls=%async_computation.7 | async-start | bytes 8912896 | tf_op jit(solution)/shard_map/all_gather | solution.py:106
  59.3 58.9 %all-to-all-start.2 = ((bf16[32,32,256]{2,1,0:T(8,128)(2,1)}), bf16[32,32,256]{2,1,0:T(8,128)(2,1)S(1)}, u32[]{:S(2)}, u32[]{:S(2)}) async-start(bf16[32,32,256]{2,1,0:T(8,128)(2,1)} %bitcast.7), calls=%async_computation.2 | async-start | bytes 1048576 | tf_op jit(solution)/shard_map/all_to_all | solution.py:65
  118.2 73.1 %all-to-all-start.3 = ((bf16[32,8,1024]{2,1,0:T(8,128)(2,1)}), bf16[32,8,1024]{2,1,0:T(8,128)(2,1)S(1)}, u32[]{:S(2)}, u32[]{:S(2)}) async-start(bf16[32,8,1024]{2,1,0:T(8,128)(2,1)} %bitcast.8), calls=%async_computation.3 | async-start | bytes 1048576 | tf_op jit(solution)/shard_map/all_to_all | solution.py:66
  196.9 42.5 %all-to-all-start.4 = ((bf16[32,2,12288]{2,1,0:T(2,128)(2,1)}), bf16[32,2,12288]{2,1,0:T(2,128)(2,1)}, u32[]{:S(2)}, u32[]{:S(2)}) async-start(bf16[32,2,12288]{2,1,0:T(2,128)(2,1)} %reshape.318), calls=%async_computation.4 | async-start | bytes 3145728 | tf_op jit(solution)/shard_map/all_to_all | solution.py:13
  280.4 1.7 copy-start
  443.9 3.4 copy-start.2
  447.3 1.0 copy-start.1
  448.4 3.0 copy-start.12
  448.4 1.4 copy-start.8
  449.4 1.9 copy-start.14
  451.3 1.0 copy-start.3
  451.3 1.1 copy-start.5
  460.4 170.8 %all-to-all-start.5 = ((bf16[16,128,1024]{2,1,0:T(8,128)(2,1)}), bf16[16,128,1024]{2,1,0:T(8,128)(2,1)}, u32[]{:S(2)}, u32[]{:S(2)}) async-start(bf16[16,128,1024]{2,1,0:T(8,128)(2,1)} %copy.25), calls=%async_computation.5 | async-start | bytes 8388608 | tf_op jit(solution)/shard_map/all_to_all | solution.py:148
  467.8 3.1 copy-start.4
  470.9 1.8 copy-start.6
  472.7 1.8 copy-start.13
  472.7 1.9 copy-start.15
Sparse Core Ops, SparseCore 0:
  11.8 210.6 all-gather.2
  226.3 189.8 all-gather.4
where the time goes:
time: 646 us; the launch traced here: 644 us
  waiting for transfers between devices  367 us (57%)
  blocking collectives  100 us (15%)
  local copies, waits for them, and re-layouts  96.8 us (15%)
  starting transfers between devices  30.6 us (5%)
  matrix products  18.4 us (3%)
  between operations  15.2 us (2%)
  other arithmetic  14.8 us (2%)
    all_to_all x1, waiting for transfers between devices, on_device(): lax.all_to_all(slots, 'group', split_axis=0, concat_axis=0, tiled=True)  155 us
    all_gather x1, waiting for transfers between devices, on_device(): tok_piece = lax.all_gather(masked_tok, 'group', axis=0, tiled=True)  134 us
    gather x108, local copies, waits for them, and re-layouts  70 us
    all_to_all x1, waiting for transfers between devices, relocate(): lax.all_to_all(down_parts, 'node', split_axis=0, concat_axis=0, tiled=True)  56.3 us
    all_gather x1, blocking collectives, on_device(): lax.all_gather(router_gate.astype(jnp.bfloat16), 'group', axis=0, tiled=T...  52.1 us
    all_to_all x1, blocking collectives, relocate(): lax.all_to_all(gate_parts, 'node', split_axis=0, concat_axis=0, tiled=True)  25.4 us
    all_to_all x1, blocking collectives, sent_to_all(): return lax.all_to_all(copies, axis, split_axis=0, concat_axis=0, tiled=True)  22.8 us
    all_to_all x1, waiting for transfers between devices, side_by_side(): lax.all_to_all(both, axis, split_axis=split_dim, concat_axis=concat_dim,...  21.4 us
  transfers between devices with their start and end apart: 6, of which 4 were waited for; matrix products, arithmetic and copies ran while one was open for 12% of the time, Pallas kernels for 0%

commit v1 on v0

--- a/solution.py
+++ b/solution.py
@@ -103,7 +103,9 @@
     wanted = sources * shard_rows + own_block * block
     column_hot = (jnp.arange(topk, dtype=jnp.int32)[None, :] == column[:, None]).astype(jnp.float32)
     empty = jnp.zeros((capacity, block, depth), jnp.bfloat16)
-    tok_piece = lax.all_gather(masked_tok, "group", axis=0, tiled=True)
+    tok_piece = jnp.concatenate(
+        lax.all_to_all(jnp.stack([masked_tok] * lax.axis_size("group")), "group", 0, 0), axis=0
+    )
     out_piece = lax.all_gather(masked_out, "group", axis=0, tiled=True)
     gate_piece = lax.all_gather(
         router_gate.astype(jnp.bfloat16), "group", axis=0, tiled=True

time: 646 us -> 845 us (1.31)
  the two profiles are of different devices: /device:TPU:36 before, /device:TPU:48 now
where the time goes in v1:
time: 845 us; the launch traced here: 843 us
  blocking collectives  469 us (56%)
  waiting for transfers between devices  182 us (22%)
  local copies, waits for them, and re-layouts  101 us (12%)
  starting transfers between devices  43.1 us (5%)
  matrix products  18.4 us (2%)
  between operations  15.2 us (2%)
  other arithmetic  13.4 us (2%)
    all_gather x1, blocking collectives, on_device(): lax.all_gather(router_gate.astype(jnp.bfloat16), 'group', axis=0, tiled=T...  422 us
    all_to_all x1, waiting for transfers between devices, on_device(): lax.all_to_all(slots, 'group', split_axis=0, concat_axis=0, tiled=True)  129 us
    gather x108, local copies, waits for them, and re-layouts  69.2 us
    all_to_all x1, waiting for transfers between devices, side_by_side(): lax.all_to_all(both, axis, split_axis=split_dim, concat_axis=concat_dim,...  35.8 us
    all_to_all x1, blocking collectives, relocate(): lax.all_to_all(gate_parts, 'node', split_axis=0, concat_axis=0, tiled=True)  26.1 us
    all_to_all x1, blocking collectives, relocate(): lax.all_to_all(up_parts, 'node', split_axis=0, concat_axis=0, tiled=True)  20.5 us
  transfers between devices with their start and end apart: 6, of which 4 were waited for; matrix products, arithmetic and copies ran while one was open for 9% of the time, Pallas kernels for 0%

profile of v1, /device:TPU:48, one launch (start us, length us, event | category | flops | bytes accessed | tf_op | source)
XLA Modules:
  0.0 842.6 jit_solution(5818984912092365314)
XLA Ops:
  7.2 26.1 %all_to_all.42 = bf16[32,32,256]{2,1,0:T(8,128)(2,1)S(1)} all-to-all(bf16[32,32,256]{2,1,0:T(8,128)(2,1)} %bitcast.95), channel_id=1, replica_groups=mesh['node'=32,'group'=16] {'node'}, dimensions={0} | all-to-all | bytes 1048576 | tf_op jit(solution)/shard_map/all_to_all | solution.py:64
  33.2 20.5 %all_to_all.43 = bf16[32,32,256]{2,1,0:T(8,128)(2,1)S(1)} all-to-all(bf16[32,32,256]{2,1,0:T(8,128)(2,1)} %bitcast.96), channel_id=1, replica_groups=mesh['node'=32,'group'=16] {'node'}, dimensions={0} | all-to-all | bytes 1048576 | tf_op jit(solution)/shard_map/all_to_all | solution.py:65
  53.8 4.6 all-to-all-start.3
  60.4 13.9 %all-to-all-done.3 = bf16[32,8,1024]{2,1,0:T(8,128)(2,1)S(1)} async-done(((bf16[32,8,1024]{2,1,0:T(8,128)(2,1)}), bf16[32,8,1024]{2,1,0:T(8,128)(2,1)S(1)}, u32[]{:S(2)}, u32[]{:S(2)}) %all-to-all-start.3) | async-done | bytes 524320 | tf_op jit(solution)/shard_map/all_to_all | solution.py:66
  74.9 12.7 %all-to-all-start = ((s32[16,1,2,4]{3,2,1,0:T(2,128)}), s32[16,1,2,4]{3,2,1,0:T(2,128)S(1)}, u32[]{:S(2)}, u32[]{:S(2)}) async-start(s32[16,1,2,4]{3,2,1,0:T(2,128)} %broadcast_in_dim.93), calls=%async_computation | async-start | bytes 32768 | tf_op jit(solution)/shard_map/all_to_all | solution.py:22
  89.3 1.9 reduce
  91.2 2.1 reshape.324
  93.3 3.4 all-to-all-done
  96.7 4.6 all-to-all-start.4
  102.9 35.8 %all-to-all-done.4 = bf16[32,2,12288]{2,1,0:T(2,128)(2,1)S(1)} async-done(((bf16[32,2,12288]{2,1,0:T(2,128)(2,1)}), bf16[32,2,12288]{2,1,0:T(2,128)(2,1)S(1)}, u32[]{:S(2)}, u32[]{:S(2)}) %all-to-all-start.4) | async-done | bytes 1572896 | tf_op jit(solution)/shard_map/all_to_all | solution.py:13
  138.8 4.3 stack.2
  143.1 8.9 %all-to-all-start.5 = ((bf16[16,256,1024]{2,1,0:T(8,128)(2,1)}), bf16[16,256,1024]{2,1,0:T(8,128)(2,1)}, u32[]{:S(2)}, u32[]{:S(2)}) async-start(bf16[16,256,1024]{2,1,0:T(8,128)(2,1)} %stack.2), calls=%async_computation.5 | async-start | bytes 16777216 | tf_op jit(solution)/shard_map/all_to_all | solution.py:107
  152.7 422.0 %all_gather.6 = bf16[4096,4]{0,1:T(4,128)(2,1)S(1)} all-gather(bf16[256,4]{0,1:T(4,128)(2,1)S(1)} %convert_element_type.78), channel_id=1, replica_groups=mesh['node'=32,'group'=16] {'group'}, dimensions={0}, use_global_device_ids=true | all-gather | bytes 34816 | tf_op jit(solution)/shard_map/all_gather | solution.py:110
  574.9 2.5 sort.17
  578.2 15.8 %while.3 = (s32[]{:T(128)}, f32[4096,4]{0,1:T(4,128)S(1)}, s32[12,2]{0,1:T(2,128)S(1)}, f32[12,128,4]{1,2,0:T(4,128)S(1)}, s32[]{:T(128)}) while((s32[]{:T(128)}, f32[4096,4]{0,1:T(4,128)S(1)}, s32[12,2]{0,1:T(2,128)S(1)}, f32[12,128,4]{1,2,0:T(4,128)S(1)}, s32[]{:T(128)}) %tuple.54), condition=%wide.while_cond, body=%wide.while_body.sunk | while | flops 2 | bytes 4193 | solution.py:121
  594.1 8.2 reshape.325
  602.3 1.7 copy.41
  607.7 26.6 %while.5 = (s32[]{:T(128)}, bf16[4096,1024]{1,0:T(8,128)(2,1)}, s32[12,2]{0,1:T(2,128)S(1)}, bf16[12,128,1024]{2,1,0:T(8,128)(2,1)S(1)}, s32[]{:T(128)}) while((s32[]{:T(128)}, bf16[4096,1024]{1,0:T(8,128)(2,1)}, s32[12,2]{0,1:T(2,128)S(1)}, bf16[12,128,1024]{2,1,0:T(8,128)(2,1)S(1)}, s32[]{:T(128)}) %tuple.65), condition=%wide.while_cond.2, body=%wide.while_body.2.sunk | while | flops 2 | bytes 524385 | solution.py:119
  608.3 1.6 bitcast_dynamic-update-slice_fusion.8
  610.5 1.6 bitcast_dynamic-update-slice_fusion.8
  612.7 1.6 bitcast_dynamic-update-slice_fusion.8
  614.9 1.6 bitcast_dynamic-update-slice_fusion.8
  617.2 1.6 bitcast_dynamic-update-slice_fusion.8
  623.8 1.6 bitcast_dynamic-update-slice_fusion.8
  634.3 1.7 copy-done
  636.4 27.4 %while.4 = (s32[]{:T(128)}, bf16[4096,1024]{1,0:T(8,128)(2,1)}, s32[12,2]{0,1:T(2,128)S(1)}, bf16[12,128,1024]{2,1,0:T(8,128)(2,1)S(1)}, s32[]{:T(128)}) while((s32[]{:T(128)}, bf16[4096,1024]{1,0:T(8,128)(2,1)}, s32[12,2]{0,1:T(2,128)S(1)}, bf16[12,128,1024]{2,1,0:T(8,128)(2,1)S(1)}, s32[]{:T(128)}) %tuple.66), condition=%wide.while_cond.1, body=%wide.while_body.1.sunk | while | flops 2 | bytes 524385 | solution.py:120
  637.0 1.7 bitcast_dynamic-update-slice_fusion.7
  639.3 1.7 bitcast_dynamic-update-slice_fusion.7
  641.6 1.7 bitcast_dynamic-update-slice_fusion.7
  643.9 1.7 bitcast_dynamic-update-slice_fusion.7
  646.1 1.7 bitcast_dynamic-update-slice_fusion.7
  648.4 1.7 bitcast_dynamic-update-slice_fusion.7
  650.7 1.7 bitcast_dynamic-update-slice_fusion.7
  653.0 1.7 bitcast_dynamic-update-slice_fusion.7
  655.3 1.7 bitcast_dynamic-update-slice_fusion.7
  657.5 1.7 bitcast_dynamic-update-slice_fusion.7
  659.8 1.7 bitcast_dynamic-update-slice_fusion.7
  662.1 1.7 bitcast_dynamic-update-slice_fusion.7
  663.8 3.4 fusion.5
  673.4 2.5 fusion.7
  675.9 4.3 copy.25
  680.3 12.3 %all-to-all-start.6 = ((bf16[16,128,1024]{2,1,0:T(8,128)(2,1)}), bf16[16,128,1024]{2,1,0:T(8,128)(2,1)}, u32[]{:S(2)}, u32[]{:S(2)}) async-start(bf16[16,128,1024]{2,1,0:T(8,128)(2,1)} %copy.25), calls=%async_computation.6 | async-start | bytes 8388608 | tf_op jit(solution)/shard_map/all_to_all | solution.py:150
  692.7 3.1 fusion.6
  695.8 1.8 fusion.15
  697.6 1.8 fusion.14
  699.5 1.9 fusion.16
  701.4 128.6 %all-to-all-done.6 = bf16[16,128,1024]{2,1,0:T(8,128)(2,1)} async-done(((bf16[16,128,1024]{2,1,0:T(8,128)(2,1)}), bf16[16,128,1024]{2,1,0:T(8,128)(2,1)}, u32[]{:S(2)}, u32[]{:S(2)}) %all-to-all-start.6) | async-done | bytes 4194336 | tf_op jit(solution)/shard_map/all_to_all | solution.py:150
  830.0 4.7 fusion.11
  (175 shorter events, 57.7 us)
Async XLA Ops:
  7.2 51.2 %copy-start.13 = (s32[32]{0:T(128)S(1)}, s32[32]{0:T(128)}, u32[]{:S(2)}) copy-start(s32[32]{0:T(128)} %param.16) | copy-start | bytes 388
  53.8 20.5 %all-to-all-start.3 = ((bf16[32,8,1024]{2,1,0:T(8,128)(2,1)}), bf16[32,8,1024]{2,1,0:T(8,128)(2,1)S(1)}, u32[]{:S(2)}, u32[]{:S(2)}) async-start(bf16[32,8,1024]{2,1,0:T(8,128)(2,1)} %bitcast.97), calls=%async_computation.3 | async-start | bytes 1048576 | tf_op jit(solution)/shard_map/all_to_all | solution.py:66
  58.4 15.9 %copy-start.12 = (s32[1,2,4]{2,1,0:T(2,128)S(1)}, s32[1,2,4]{2,1,0:T(2,128)}, u32[]{:S(2)}) copy-start(s32[1,2,4]{2,1,0:T(2,128)} %param.15) | copy-start | bytes 100
  74.9 21.8 %all-to-all-start = ((s32[16,1,2,4]{3,2,1,0:T(2,128)}), s32[16,1,2,4]{3,2,1,0:T(2,128)S(1)}, u32[]{:S(2)}, u32[]{:S(2)}) async-start(s32[16,1,2,4]{3,2,1,0:T(2,128)} %broadcast_in_dim.93), calls=%async_computation | async-start | bytes 32768 | tf_op jit(solution)/shard_map/all_to_all | solution.py:22
  93.3 8.7 %copy-start.8 = (bf16[256,1024]{1,0:T(8,128)(2,1)S(1)}, bf16[256,1024]{1,0:T(8,128)(2,1)}, u32[]{:S(2)}) copy-start(bf16[256,1024]{1,0:T(8,128)(2,1)} %param.12) | copy-start | bytes 1572868
  93.3 8.7 %copy-start.9 = (bf16[256,1024]{1,0:T(8,128)(2,1)S(1)}, bf16[256,1024]{1,0:T(8,128)(2,1)}, u32[]{:S(2)}) copy-start(bf16[256,1024]{1,0:T(8,128)(2,1)} %param.11) | copy-start | bytes 1572868
  96.7 42.1 %all-to-all-start.4 = ((bf16[32,2,12288]{2,1,0:T(2,128)(2,1)}), bf16[32,2,12288]{2,1,0:T(2,128)(2,1)S(1)}, u32[]{:S(2)}, u32[]{:S(2)}) async-start(bf16[32,2,12288]{2,1,0:T(2,128)(2,1)} %reshape.324), calls=%async_computation.4 | async-start | bytes 3145728 | tf_op jit(solution)/shard_map/all_to_all | solution.py:13
  138.8 4.3 copy-start.1
  143.1 9.6 %copy-start.11 = (f32[256,4]{0,1:T(4,128)S(1)}, f32[256,4]{0,1:T(4,128)}, u32[]{:S(2)}) copy-start(f32[256,4]{0,1:T(4,128)} %param.13) | copy-start | bytes 12292
  143.1 464.2 %all-to-all-start.5 = ((bf16[16,256,1024]{2,1,0:T(8,128)(2,1)}), bf16[16,256,1024]{2,1,0:T(8,128)(2,1)}, u32[]{:S(2)}, u32[]{:S(2)}) async-start(bf16[16,256,1024]{2,1,0:T(8,128)(2,1)} %stack.2), calls=%async_computation.5 | async-start | bytes 16777216 | tf_op jit(solution)/shard_map/all_to_all | solution.py:107
  152.0 484.0 %all-gather.2.cloned.1.call-start = ((), (), s32[]{:S(2)}) async-start(), calls=%async_computation.7 | async-start | bytes 8912896 | tf_op jit(solution)/shard_map/all_gather | solution.py:109
  634.3 1.7 copy-start
  663.8 3.4 copy-start.3
  667.2 1.0 copy-start.2
  668.2 3.0 copy-start.14
  668.2 1.4 copy-start.10
  669.2 1.9 copy-start.16
  671.2 1.0 copy-start.4
  671.2 1.2 copy-start.6
  680.3 149.8 %all-to-all-start.6 = ((bf16[16,128,1024]{2,1,0:T(8,128)(2,1)}), bf16[16,128,1024]{2,1,0:T(8,128)(2,1)}, u32[]{:S(2)}, u32[]{:S(2)}) async-start(bf16[16,128,1024]{2,1,0:T(8,128)(2,1)} %copy.25), calls=%async_computation.6 | async-start | bytes 8388608 | tf_op jit(solution)/shard_map/all_to_all | solution.py:150
  692.7 3.1 copy-start.7
  695.8 1.8 copy-start.5
  697.6 1.8 copy-start.15
  697.6 1.9 copy-start.17
Sparse Core Ops, SparseCore 0:
  156.6 399.4 all-gather.1
